TPU v7x, 32 devices: a whole 2x2x4 slice. The times are simulated.
32 devices in a mesh: dp: 4 (over x, core), head: 4 (over z), expert: 2 (over y).
Axes of the slice: x: 2, y: 2, z: 4, core: 2. Of those that a mesh axis runs over, the one named last changes fastest.
Arguments:
- tokens: bfloat16 [4, 64, 4096], P('dp', ('head', 'expert')), may hold values from -6 to 6
- cotangent: bfloat16 [4, 64, 4096], P('dp', ('head', 'expert')), may hold values from -1.5 to 1.5
- queries: bfloat16 [4, 64, 32, 128], P('dp', 'expert', 'head'), may hold values from -32 to 32
- key_vectors: bfloat16 [4, 64, 32, 128], P('dp', 'expert', 'head'), may hold values from -32 to 32
- value_routes: int32 [4, 32, 64, 1], P('dp', 'head'), may hold values from 0 to 3; in each aligned block of 8 rows (0 to 7, 8 to 15, ..., all dimensions but the last counted through in order) at most 3 rows name the same one
- output_routes: int32 [4, 32, 64, 1], P('dp', 'head'), may hold values from 0 to 3; in each aligned block of 8 rows (0 to 7, 8 to 15, ..., all dimensions but the last counted through in order) at most 3 rows name the same one
- value_experts: bfloat16 [128, 4096, 128], P(('head', 'expert')), may hold values from -0.09375 to 0.09375
- output_experts: bfloat16 [128, 4096, 128], P(('head', 'expert')), may hold values from -0.09375 to 0.09375
Outputs:
- token_grads: bfloat16 [4, 64, 4096], P('dp', ('head', 'expert'))
- query_grads: bfloat16 [4, 64, 32, 128], P('dp', 'expert', 'head')
- key_grads: bfloat16 [4, 64, 32, 128], P('dp', 'expert', 'head')
- value_grads: bfloat16 [128, 4096, 128], P(('head', 'expert'), 'dp')
- output_grads: bfloat16 [128, 4096, 128], P(('head', 'expert'), 'dp')
Inputs may be any that keep to these rules, and one draw needn't show every extreme that they name: value_routes[b, h, t, 0] is the value expert of head h for token t. In each aligned block of 8 tokens of one sequence and head, no expert is chosen more than 3 times, and in every draw some block has exactly 3 for one expert. output_routes[b, h, t, 0] is the output expert of head h for token t. In each aligned block of 8 tokens of one sequence and head, no expert is chosen more than 3 times, and in every draw some block has exactly 3 for one expert.
All inputs are finite; a program needn't handle non-finite values.
Results may differ from a plain program's by a relative error of at most 0.028.
Values may be sent and summed in bfloat16 or wider, within the bound.
A program may use at most 128 MiB of HBM per device.

v0:
```python
import jax
import jax.numpy as jnp
from jax import lax
from jax.sharding import PartitionSpec as P

E = 4
CAP = 3


def slot_rank(routes):
    onehot = (routes[..., None] == jnp.arange(E, dtype=jnp.int32)).astype(jnp.int32)
    before = jnp.cumsum(onehot, axis=-2) - onehot
    return jnp.sum(before * onehot, axis=-1)


def slot_table(routes):
    rank_of = slot_rank(routes)
    expert_hit = routes[..., None, None, :] == jnp.arange(E, dtype=jnp.int32)[:, None, None]
    place_hit = rank_of[..., None, None, :] == jnp.arange(CAP, dtype=jnp.int32)[:, None]
    return jnp.logical_and(expert_hit, place_hit).astype(jnp.bfloat16)


def local(
    tokens,
    cotangent,
    queries,
    key_vectors,
    value_routes,
    output_routes,
    value_experts,
    output_experts,
):
    head_count = lax.axis_size("head")
    expert_count = lax.axis_size("expert")
    sources = head_count * expert_count
    expert_index = lax.axis_index("expert")
    tok_rows = tokens.shape[1]
    model_width = tokens.shape[2]
    query_rows = queries.shape[1]
    groups = queries.shape[2]
    head_dim = queries.shape[3]
    seq_len = value_routes.shape[2]
    pairs_dev = value_experts.shape[0]
    slot_count = sources * CAP
    score_scale = head_dim ** (-0.5)
    value_local = value_routes[0, :, :, 0]
    output_local = output_routes[0, :, :, 0]

    def own_block(route_part):
        shaped = route_part.reshape(groups, head_count, expert_count, tok_rows)
        return lax.dynamic_index_in_dim(shaped, expert_index, 2, keepdims=False)

    own_pair = jnp.stack([own_block(value_local), own_block(output_local)])
    own_routes = lax.all_to_all(own_pair, "head", split_axis=2, concat_axis=1, tiled=True).reshape(
        2, groups * head_count, tok_rows
    )
    value_table = slot_table(own_routes[0]).reshape(
        head_count, expert_count, pairs_dev, CAP, tok_rows
    )

    def pair_rows(route_part, gathered):
        slot_map = slot_table(route_part.reshape(groups, sources, tok_rows))
        slot_map = jnp.moveaxis(slot_map, 2, 1).reshape(groups * E, sources, CAP, tok_rows)
        slot_map = lax.dynamic_slice_in_dim(slot_map, expert_index * pairs_dev, pairs_dev, 0)
        picked = jnp.einsum(
            "psmt,stw->psmw",
            slot_map,
            gathered.reshape(sources, tok_rows, model_width),
            preferred_element_type=jnp.float32,
        )
        return picked.astype(jnp.bfloat16).reshape(pairs_dev, slot_count, model_width)

    whole_tokens, whole_cotangent = (
        lax.all_gather(tokens[0], ("head", "expert"), axis=0, tiled=True),
        lax.all_gather(cotangent[0], ("head", "expert"), axis=0, tiled=True),
    )
    token_slots = pair_rows(value_local, whole_tokens)
    cotangent_slots = pair_rows(output_local, whole_cotangent)
    value_slots = jnp.einsum(
        "prw,pwk->prk", token_slots, value_experts, preferred_element_type=jnp.float32
    ).astype(jnp.bfloat16)
    upstream_slots = jnp.einsum(
        "prw,pwk->prk", cotangent_slots, output_experts, preferred_element_type=jnp.float32
    ).astype(jnp.bfloat16)
    query_start = expert_index * query_rows
    group_values, group_upstream, all_keys = (
        lax.all_gather(value_slots, "expert", axis=0, tiled=True),
        lax.all_gather(upstream_slots, "expert", axis=0, tiled=True),
        lax.all_gather(key_vectors[0], "expert", axis=0, tiled=True),
    )
    token_source = jnp.arange(seq_len, dtype=jnp.int32) // tok_rows
    head_base = jnp.arange(groups, dtype=jnp.int32)[:, None] * E
    value_rank = slot_rank(value_local.reshape(groups, sources, tok_rows)).reshape(groups, seq_len)
    value_index = (head_base + value_local) * slot_count + token_source * CAP + value_rank
    value_rows = group_values.reshape(-1, head_dim)[value_index]
    output_rank = slot_rank(output_local.reshape(groups, sources, tok_rows)).reshape(
        groups, seq_len
    )
    block_routes = lax.dynamic_slice_in_dim(output_local, query_start, query_rows, 1)
    block_rank = lax.dynamic_slice_in_dim(output_rank, query_start, query_rows, 1)
    block_source = lax.dynamic_slice_in_dim(token_source, query_start, query_rows, 0)
    upstream_index = (head_base + block_routes) * slot_count + block_source * CAP + block_rank
    upstream_rows = group_upstream.reshape(-1, head_dim)[upstream_index]
    query_own = queries[0]
    scores = (
        jnp.einsum("ihc,jhc->hij", query_own, all_keys, preferred_element_type=jnp.float32)
        * score_scale
    )
    query_pos = query_start + jnp.arange(query_rows, dtype=jnp.int32)
    causal = jnp.arange(seq_len, dtype=jnp.int32)[None, :] <= query_pos[:, None]
    row_top = jnp.max(jnp.where(causal, scores, -jnp.inf), axis=-1, keepdims=True)
    weights = jnp.where(causal, jnp.exp(scores - row_top), 0.0)
    probs_full = weights / jnp.sum(weights, axis=-1, keepdims=True)
    prob_half = probs_full.astype(jnp.bfloat16)
    outputs = jnp.einsum(
        "hij,hjc->hic", prob_half, value_rows, preferred_element_type=jnp.float32
    ).astype(jnp.bfloat16)
    row_delta = jnp.sum(outputs.astype(jnp.float32) * upstream_rows.astype(jnp.float32), axis=-1)
    prob_grads = jnp.einsum(
        "hic,hjc->hij", upstream_rows, value_rows, preferred_element_type=jnp.float32
    )
    score_grads = (probs_full * (prob_grads - row_delta[:, :, None])).astype(jnp.bfloat16)
    query_grads = (
        jnp.einsum("hij,jhc->ihc", score_grads, all_keys, preferred_element_type=jnp.float32)
        * score_scale
    ).astype(jnp.bfloat16)
    key_part = (
        jnp.einsum("hij,ihc->jhc", score_grads, query_own, preferred_element_type=jnp.float32)
        * score_scale
    )
    value_part = jnp.einsum(
        "hij,hic->jhc", prob_half, upstream_rows, preferred_element_type=jnp.float32
    )
    key_sum, value_sum = (
        lax.psum_scatter(key_part, "expert", scatter_dimension=0, tiled=True),
        lax.psum_scatter(value_part, "expert", scatter_dimension=0, tiled=True),
    )
    value_half = value_sum.astype(jnp.bfloat16)
    block_value_routes = lax.dynamic_slice_in_dim(value_local, query_start, query_rows, 1).reshape(
        groups, head_count, tok_rows
    )
    value_place = slot_table(block_value_routes)
    output_place = slot_table(block_routes.reshape(groups, head_count, tok_rows))
    value_send = jnp.einsum(
        "hsemt,sthc->hesmc",
        value_place,
        value_half.reshape(head_count, tok_rows, groups, head_dim),
        preferred_element_type=jnp.float32,
    )
    value_send = value_send.astype(jnp.bfloat16).reshape(groups * E, head_count * CAP, head_dim)
    output_send = jnp.einsum(
        "hsemt,hstc->hesmc",
        output_place,
        outputs.reshape(groups, head_count, tok_rows, head_dim),
        preferred_element_type=jnp.float32,
    )
    output_send = output_send.astype(jnp.bfloat16).reshape(groups * E, head_count * CAP, head_dim)
    output_slots, grad_slots = (
        lax.all_to_all(output_send, "expert", split_axis=0, concat_axis=1, tiled=True),
        lax.all_to_all(value_send, "expert", split_axis=0, concat_axis=1, tiled=True),
    )
    value_term = jnp.einsum(
        "prw,prk->pwk", token_slots, grad_slots, preferred_element_type=jnp.float32
    )
    output_term = jnp.einsum(
        "prw,prk->pwk", cotangent_slots, output_slots, preferred_element_type=jnp.float32
    )
    value_grads, output_grads = (
        lax.psum_scatter(
            value_term.astype(jnp.bfloat16), "dp", scatter_dimension=1, tiled=True
        ).astype(jnp.float32),
        lax.psum_scatter(
            output_term.astype(jnp.bfloat16), "dp", scatter_dimension=1, tiled=True
        ).astype(jnp.float32),
    )
    token_terms = jnp.einsum(
        "prk,pwk->prw", grad_slots, value_experts, preferred_element_type=jnp.float32
    ).astype(jnp.bfloat16)
    returned = lax.all_to_all(
        token_terms.reshape(pairs_dev, sources, CAP, model_width),
        ("head", "expert"),
        split_axis=1,
        concat_axis=0,
        tiled=True,
    )
    returned = returned.reshape(head_count, expert_count, pairs_dev, CAP, model_width)
    token_grads = jnp.einsum(
        "gjpmt,gjpmw->tw", value_table, returned, preferred_element_type=jnp.float32
    )
    return (
        token_grads.astype(jnp.bfloat16)[None],
        query_grads[None],
        key_sum.astype(jnp.bfloat16)[None],
        value_grads.astype(jnp.bfloat16),
        output_grads.astype(jnp.bfloat16),
    )


def exchanged(
    tokens,
    cotangent,
    queries,
    key_vectors,
    value_routes,
    output_routes,
    value_experts,
    output_experts,
):
    dp_count = lax.axis_size("dp")
    dp_index = lax.axis_index("dp")
    expert_count = lax.axis_size("expert")
    expert_index = lax.axis_index("expert")
    sources = lax.axis_size("head") * expert_count
    tok_rows = tokens.shape[1]
    width = tokens.shape[2] // dp_count
    groups = queries.shape[2]
    head_dim = queries.shape[3]
    seq_len = value_routes.shape[2]
    pairs_dev = value_experts.shape[0]
    own_heads = groups // expert_count
    score_scale = head_dim ** (-0.5)
    rows = jnp.stack([tokens[0], cotangent[0]])
    rows = lax.all_to_all(rows, "dp", split_axis=2, concat_axis=1, tiled=True)
    rows = lax.all_gather(
        rows.reshape(2, dp_count, tok_rows, width), ("head", "expert"), axis=2, tiled=True
    )
    token_rows = rows[0].reshape(dp_count * seq_len, width)
    cotangent_rows = rows[1].reshape(dp_count * seq_len, width)
    routes = jnp.stack([value_routes[0, :, :, 0], output_routes[0, :, :, 0]])
    routes = lax.dynamic_slice_in_dim(routes, expert_index * own_heads, own_heads, 1)
    routes = lax.all_gather(routes, "dp", axis=1)
    picks = jnp.moveaxis(routes, 3, 2)[..., None] == jnp.arange(E, dtype=jnp.int32)
    picks = picks.reshape(2, dp_count * seq_len, own_heads, E, 1)
    pair = jnp.stack([queries[0], key_vectors[0]])
    pair = lax.all_to_all(pair, "expert", split_axis=2, concat_axis=1, tiled=True)
    query_all, key_all = (pair[0], pair[1])
    value_weight = lax.dynamic_slice_in_dim(value_experts, dp_index * width, width, 1)
    output_weight = lax.dynamic_slice_in_dim(output_experts, dp_index * width, width, 1)

    def project(source_rows, weight, pick):
        every = jnp.einsum("td,pdk->tpk", source_rows, weight, preferred_element_type=jnp.float32)
        every = every.reshape(dp_count * seq_len, own_heads, E, head_dim)
        return jnp.sum(jnp.where(pick, every, 0.0), axis=2).astype(jnp.bfloat16)

    part = jnp.stack(
        [
            project(token_rows, value_weight, picks[0]).reshape(
                dp_count, seq_len, own_heads, head_dim
            ),
            project(cotangent_rows, output_weight, picks[1]).reshape(
                dp_count, seq_len, own_heads, head_dim
            ),
        ],
        axis=1,
    )
    part = lax.all_to_all(part, "dp", split_axis=0, concat_axis=0, tiled=True)
    whole = jnp.sum(part.astype(jnp.float32), axis=0).astype(jnp.bfloat16)
    values, upstream = (whole[0], whole[1])
    scores = (
        jnp.einsum("ihc,jhc->hij", query_all, key_all, preferred_element_type=jnp.float32)
        * score_scale
    )
    position = jnp.arange(seq_len, dtype=jnp.int32)
    causal = position[None, :] <= position[:, None]
    row_top = jnp.max(jnp.where(causal, scores, -jnp.inf), axis=-1, keepdims=True)
    weights = jnp.where(causal, jnp.exp(scores - row_top), 0.0)
    probs = weights / jnp.sum(weights, axis=-1, keepdims=True)
    prob_half = probs.astype(jnp.bfloat16)
    outputs = jnp.einsum(
        "hij,jhc->ihc", prob_half, values, preferred_element_type=jnp.float32
    ).astype(jnp.bfloat16)
    row_delta = jnp.sum(outputs.astype(jnp.float32) * upstream.astype(jnp.float32), axis=-1)
    prob_grads = jnp.einsum("ihc,jhc->hij", upstream, values, preferred_element_type=jnp.float32)
    value_half = jnp.einsum(
        "hij,ihc->jhc", prob_half, upstream, preferred_element_type=jnp.float32
    ).astype(jnp.bfloat16)
    score_grads = (probs * (prob_grads - row_delta.T[:, :, None])).astype(jnp.bfloat16)
    query_grads = (
        jnp.einsum("hij,jhc->ihc", score_grads, key_all, preferred_element_type=jnp.float32)
        * score_scale
    ).astype(jnp.bfloat16)
    key_grads = (
        jnp.einsum("hij,ihc->jhc", score_grads, query_all, preferred_element_type=jnp.float32)
        * score_scale
    ).astype(jnp.bfloat16)
    factors = lax.all_gather(jnp.stack([value_half, outputs]), "dp", axis=1)
    factors = factors.reshape(2, dp_count * seq_len, own_heads, 1, head_dim)
    factors = jnp.where(picks, factors, jnp.zeros((), jnp.bfloat16)).reshape(
        2, dp_count * seq_len, pairs_dev, head_dim
    )
    token_part = jnp.einsum(
        "tpk,pdk->td", factors[0], value_weight, preferred_element_type=jnp.float32
    ).astype(jnp.bfloat16)
    token_part = lax.all_to_all(
        token_part.reshape(dp_count * sources, tok_rows, width),
        ("dp", "head", "expert"),
        split_axis=0,
        concat_axis=0,
        tiled=True,
    )
    token_grads = jnp.sum(
        token_part.reshape(dp_count, sources, tok_rows, width).astype(jnp.float32), axis=1
    ).astype(jnp.bfloat16)
    token_grads = jnp.moveaxis(token_grads, 0, 1).reshape(tok_rows, dp_count * width)
    value_grads = jnp.einsum(
        "td,tpk->pdk", token_rows, factors[0], preferred_element_type=jnp.float32
    ).astype(jnp.bfloat16)
    output_grads = jnp.einsum(
        "td,tpk->pdk", cotangent_rows, factors[1], preferred_element_type=jnp.float32
    ).astype(jnp.bfloat16)
    back = lax.all_to_all(
        jnp.stack([query_grads, key_grads]), "expert", split_axis=1, concat_axis=2, tiled=True
    )
    return (token_grads[None], back[0][None], back[1][None], value_grads, output_grads)


def chosen(*args):
    groups, pairs_dev = (args[2].shape[2], args[6].shape[0])
    expert_count = lax.axis_size("expert")
    whole_heads = groups % expert_count == 0 and pairs_dev == groups // expert_count * E
    if whole_heads and args[0].shape[2] % (lax.axis_size("dp") * 128) == 0:
        return exchanged(*args)
    return local(*args)


def solution(mesh):
    return jax.shard_map(
        chosen,
        mesh=mesh,
        in_specs=(
            P("dp", ("head", "expert"), None),
            P("dp", ("head", "expert"), None),
            P("dp", "expert", "head", None),
            P("dp", "expert", "head", None),
            P("dp", "head", None, None),
            P("dp", "head", None, None),
            P(("head", "expert"), None, None),
            P(("head", "expert"), None, None),
        ),
        out_specs=(
            P("dp", ("head", "expert"), None),
            P("dp", "expert", "head", None),
            P("dp", "expert", "head", None),
            P(("head", "expert"), "dp", None),
            P(("head", "expert"), "dp", None),
        ),
        check_vma=False,
    )
```

profile of v0, /device:TPU:0, one launch (start us, length us, event | category | flops | bytes accessed | tf_op | source)
XLA Modules:
  0.0 138.1 jit_solution(9172476691813793022)
XLA Ops:
  8.1 2.8 %copy.61 = bf16[2,8,4096]{1,0,2:T(2,128)(2,1)S(1)} copy(bf16[2,8,4096]{2,1,0:T(8,128)(2,1)S(1)} %pad_maximum_fusion.2) | data formatting | bytes 262144 | tf_op jit(solution)/shard_map/stack | solution.py:222
  10.9 2.2 %reshape.83 = bf16[4,2,8192]{2,1,0:T(2,128)(2,1)S(1)} reshape(bf16[4096,2,8]{2,1,0:T(2,128)(2,1)S(1)} %bitcast.116) | data formatting | bytes 262144
  13.2 8.6 %all_to_all.55 = bf16[4,2,8192]{2,1,0:T(2,128)(2,1)S(1)} all-to-all(bf16[4,2,8192]{2,1,0:T(2,128)(2,1)S(1)} %reshape.83), channel_id=1, replica_groups=mesh['dp'=4,'head'=4,'expert'=2] {'dp'}, dimensions={0} | all-to-all | bytes 262144 | tf_op jit(solution)/shard_map/all_to_all | solution.py:223
  21.8 2.4 %reshape.84 = bf16[4096,2,8]{2,1,0:T(2,128)(2,1)S(1)} reshape(bf16[4,2,8192]{2,1,0:T(2,128)(2,1)S(1)} %all_to_all.55) | data formatting | bytes 262144
  24.2 3.2 %copy.62 = bf16[2,8,4,1024]{3,1,2,0:T(8,128)(2,1)} copy(bf16[2,8,4,1024]{1,0,3,2:T(2,128)(2,1)S(1)} %bitcast.117) | data formatting | bytes 262144 | tf_op jit(solution)/shard_map/all_to_all | solution.py:223
  28.2 3.4 %all-to-all-start.2 = ((bf16[2,32,8,128]{3,1,0,2:T(8,128)(2,1)}), bf16[2,32,8,128]{3,1,0,2:T(8,128)(2,1)S(1)}, u32[]{:S(2)}, u32[]{:S(2)}) async-start(bf16[2,32,8,128]{3,1,0,2:T(8,128)(2,1)} %pad_maximum_fusion.1), calls=%async_computation.2 | async-start | bytes 262144 | tf_op jit(solution)/shard_map/all_to_all | solution.py:235
  31.6 5.2 %all-gather = s32[2,16,64]{2,0,1:T(2,128)S(1)} all-gather(s32[2,4,64]{2,0,1:T(2,128)S(1)} %fusion.17), channel_id=2, replica_groups=mesh['dp'=4,'head'=4,'expert'=2] {'dp'}, dimensions={1}, use_global_device_ids=true | all-gather | bytes 10240 | tf_op jit(solution)/shard_map/all_gather | solution.py:231
  37.2 7.8 %constant_dynamic-slice_fusion = (bf16[16,1024,128]{2,1,0:T(8,128)(2,1)}, bf16[16,1024,128]{2,1,0:T(8,128)(2,1)}) fusion(bf16[16,4096,128]{2,1,0:T(8,128)(2,1)} %param.15, s32[]{:T(128)S(6)} %select_n.26, bf16[16,4096,128]{2,1,0:T(8,128)(2,1)} %param.14), kind=kLoop, calls=%fused_computation.48 | loop fusion | bytes 16777220 | tf_op jit(solution)/shard_map/dynamic_slice | solution.py:238
  45.0 23.2 %all-gather.4.cloned.1.call-done = bf16[2,4,64,1024]{3,2,1,0:T(8,128)(2,1)} async-done(((bf16[2,4,8,1024]{3,2,1,0:T(8,128)(2,1)}), bf16[2,4,64,1024]{3,2,1,0:T(8,128)(2,1)}) %all-gather.4.cloned.1.call-update) | async-done | bytes 1048592 | tf_op jit(solution)/shard_map/all_gather | solution.py:224
  68.2 1.3 fusion.30
  69.5 3.3 %select_reduce_fusion = bf16[256,4,128]{2,0,1:T(8,128)(2,1)S(1)} fusion(bf16[256,1024,1,1]{1,0,3,2:T(8,128)(2,1)S(1)} %bitcast.125, bf16[4,4,128,1024]{2,3,1,0:T(8,128)(2,1)} %bitcast.119, pred[256,4,4]{0,2,1:T(4,128)(4,1)S(1)} %broadcast_in_dim.69), kind=kOutput, calls=%fused_computation.3 | convolution fusion | flops 1074659328 | bytes 4984832 | tf_op jit(solution)/shard_map/td,pdk->tpk/dot_general | solution.py:241
  73.2 1.5 %select_reduce_fusion.1 = bf16[256,4,128]{2,0,1:T(8,128)(2,1)S(1)} fusion(bf16[256,1024,1,1]{1,0,3,2:T(8,128)(2,1)S(1)} %bitcast.123, bf16[4,4,128,1024]{2,3,1,0:T(8,128)(2,1)S(1)} %bitcast.118, pred[256,4,4]{0,2,1:T(4,128)(4,1)S(1)} %broadcast_in_dim.66), kind=kOutput, calls=%fused_computation.4 | convolution fusion | flops 1074659328 | bytes 4984832 | tf_op jit(solution)/shard_map/td,pdk->tpk/dot_general | solution.py:241
  75.0 1.1 pad_maximum_fusion
  76.1 3.5 %all-to-all-start.1 = ((bf16[4,2,64,4,128]{4,3,2,1,0:T(4,128)(2,1)}), bf16[4,2,64,4,128]{4,3,2,1,0:T(4,128)(2,1)S(1)}, u32[]{:S(2)}, u32[]{:S(2)}) async-start(bf16[4,2,64,4,128]{4,3,2,1,0:T(4,128)(2,1)} %pad_maximum_fusion), calls=%async_computation.1 | async-start | bytes 1048576 | tf_op jit(solution)/shard_map/all_to_all | solution.py:256
  79.8 8.5 %all-to-all-done.1 = bf16[4,2,64,4,128]{4,3,2,1,0:T(4,128)(2,1)S(1)} async-done(((bf16[4,2,64,4,128]{4,3,2,1,0:T(4,128)(2,1)}), bf16[4,2,64,4,128]{4,3,2,1,0:T(4,128)(2,1)S(1)}, u32[]{:S(2)}, u32[]{:S(2)}) %all-to-all-start.1) | async-done | bytes 524320 | tf_op jit(solution)/shard_map/all_to_all | solution.py:256
  90.6 3.4 %all-to-all-start.4 = ((bf16[2,64,4,128]{3,2,0,1:T(4,128)(2,1)}), bf16[2,64,4,128]{3,2,0,1:T(4,128)(2,1)S(1)}, u32[]{:S(2)}, u32[]{:S(2)}) async-start(bf16[2,64,4,128]{3,2,0,1:T(4,128)(2,1)} %copy.75), calls=%async_computation.4 | async-start | bytes 262144 | tf_op jit(solution)/shard_map/all_to_all | solution.py:311
  94.0 6.6 %all-gather.1 = bf16[2,256,4,128]{3,1,2,0:T(8,128)(2,1)S(1)} all-gather(bf16[2,64,4,128]{3,1,2,0:T(8,128)(2,1)S(1)} %pad_maximum_fusion.3), channel_id=3, replica_groups=mesh['dp'=4,'head'=4,'expert'=2] {'dp'}, dimensions={1}, use_global_device_ids=true | all-gather | bytes 655360 | tf_op jit(solution)/shard_map/all_gather | solution.py:286
  100.6 1.4 %broadcast_select_fusion = bf16[2,256,4,4,128]{4,1,3,2,0:T(8,128)(2,1)S(1)} fusion(pred[2,256,4,4]{1,3,2,0:T(4,128)(4,1)S(1)} %iota_compare_fusion.2, bf16[2,256,4,128]{3,1,2,0:T(8,128)(2,1)S(1)} %all-gather.1), kind=kLoop, calls=%fused_computation.5 | loop fusion | flops 1048576 | bytes 2629632 | tf_op jit(solution)/shard_map/jit(_where)/select_n | solution.py:288
  102.2 2.1 %fusion.2 = bf16[32,8,1024]{2,1,0:T(8,128)(2,1)} fusion(bf16[256,16,128]{2,0,1:T(8,128)(2,1)S(1)} %bitcast.120, bf16[16,1024,128]{2,1,0:T(8,128)(2,1)S(1)} %copy-done.1), kind=kOutput, calls=%fused_computation.8 | convolution fusion | flops 1074003968 | bytes 5767168 | tf_op jit(solution)/shard_map/tpk,pdk->td/dot_general | solution.py:291
  104.3 4.6 %all-to-all-start.3 = ((bf16[32,8,1024]{2,1,0:T(8,128)(2,1)}), bf16[32,8,1024]{2,1,0:T(8,128)(2,1)S(1)}, u32[]{:S(2)}, u32[]{:S(2)}) async-start(bf16[32,8,1024]{2,1,0:T(8,128)(2,1)} %fusion.2), calls=%async_computation.3 | async-start | bytes 1048576 | tf_op jit(solution)/shard_map/all_to_all | solution.py:294
  108.9 4.3 %convert_bitcast_fusion = bf16[16,1024,128]{1,2,0:T(8,128)(2,1)} fusion(bf16[256,16,128]{2,0,1:T(8,128)(2,1)S(1)} %bitcast.122, bf16[256,1024,1]{1,0,2:T(8,128)(2,1)} %bitcast.126), kind=kOutput, calls=%fused_computation.1 | convolution fusion | flops 1075838976 | bytes 5767168 | tf_op jit(solution)/shard_map/td,tpk->pdk/dot_general | solution.py:308
  113.3 6.4 %copy.81 = bf16[16,1024,128]{2,1,0:T(8,128)(2,1)} copy(bf16[16,1024,128]{1,2,0:T(8,128)(2,1)} %convert_bitcast_fusion) | data formatting | bytes 8388608
  119.6 3.2 %convert_bitcast_fusion.1 = bf16[16,1024,128]{1,2,0:T(8,128)(2,1)} fusion(bf16[256,16,128]{2,0,1:T(8,128)(2,1)S(1)} %bitcast.121, bf16[256,1024,1]{1,0,2:T(8,128)(2,1)S(1)} %bitcast.124), kind=kOutput, calls=%fused_computation.2 | convolution fusion | flops 1075838976 | bytes 5767168 | tf_op jit(solution)/shard_map/td,tpk->pdk/dot_general | solution.py:305
  122.9 6.4 %copy.80 = bf16[16,1024,128]{2,1,0:T(8,128)(2,1)} copy(bf16[16,1024,128]{1,2,0:T(8,128)(2,1)} %convert_bitcast_fusion.1) | data formatting | bytes 8388608
  (53 shorter events, 7.1 us)
Async XLA Ops:
  7.2 61.1 %all-gather.4.cloned.1.call-start = ((), (), s32[]{:S(2)}) async-start(), calls=%async_computation.5 | async-start | bytes 1179648 | tf_op jit(solution)/shard_map/all_gather | solution.py:224
  8.1 19.4 %copy-start.3 = (bf16[1,32,8,128]{3,2,1,0:T(8,128)(2,1)S(1)}, bf16[1,32,8,128]{3,2,1,0:T(8,128)(2,1)}, u32[]{:S(2)}) copy-start(bf16[1,32,8,128]{3,2,1,0:T(8,128)(2,1)} %param.10) | copy-start | bytes 196612
  8.1 19.4 %copy-start.4 = (bf16[1,32,8,128]{3,2,1,0:T(8,128)(2,1)S(1)}, bf16[1,32,8,128]{3,2,1,0:T(8,128)(2,1)}, u32[]{:S(2)}) copy-start(bf16[1,32,8,128]{3,2,1,0:T(8,128)(2,1)} %param.11) | copy-start | bytes 196612
  10.9 20.7 %copy-start.5 = (s32[1,8,64,1]{2,3,1,0:T(1,128)S(1)}, s32[1,8,64,1]{2,3,1,0:T(1,128)}, u32[]{:S(2)}) copy-start(s32[1,8,64,1]{2,3,1,0:T(1,128)} %param.12) | copy-start | bytes 6148
  10.9 20.7 %copy-start.6 = (s32[1,8,64,1]{2,3,1,0:T(1,128)S(1)}, s32[1,8,64,1]{2,3,1,0:T(1,128)}, u32[]{:S(2)}) copy-start(s32[1,8,64,1]{2,3,1,0:T(1,128)} %param.13) | copy-start | bytes 6148
  28.2 16.8 %all-to-all-start.2 = ((bf16[2,32,8,128]{3,1,0,2:T(8,128)(2,1)}), bf16[2,32,8,128]{3,1,0,2:T(8,128)(2,1)S(1)}, u32[]{:S(2)}, u32[]{:S(2)}) async-start(bf16[2,32,8,128]{3,1,0,2:T(8,128)(2,1)} %pad_maximum_fusion.1), calls=%async_computation.2 | async-start | bytes 262144 | tf_op jit(solution)/shard_map/all_to_all | solution.py:235
  69.5 5.2 %copy-start.2 = (bf16[1,4,64,1024]{3,2,1,0:T(8,128)(2,1)}, bf16[1,4,64,1024]{3,2,1,0:T(8,128)(2,1)S(1)}, u32[]{:S(2)}) copy-start(bf16[1,4,64,1024]{3,2,1,0:T(8,128)(2,1)S(1)} %get-tuple-element.28) | copy-start | bytes 1572868
  69.5 3.6 %copy-start = (bf16[16,1024,128]{2,1,0:T(8,128)(2,1)S(1)}, bf16[16,1024,128]{2,1,0:T(8,128)(2,1)}, u32[]{:S(2)}) copy-start(bf16[16,1024,128]{2,1,0:T(8,128)(2,1)} %get-tuple-element.42) | copy-start | bytes 12582916
  76.1 12.3 %all-to-all-start.1 = ((bf16[4,2,64,4,128]{4,3,2,1,0:T(4,128)(2,1)}), bf16[4,2,64,4,128]{4,3,2,1,0:T(4,128)(2,1)S(1)}, u32[]{:S(2)}, u32[]{:S(2)}) async-start(bf16[4,2,64,4,128]{4,3,2,1,0:T(4,128)(2,1)} %pad_maximum_fusion), calls=%async_computation.1 | async-start | bytes 1048576 | tf_op jit(solution)/shard_map/all_to_all | solution.py:256
  90.6 13.7 %all-to-all-start.4 = ((bf16[2,64,4,128]{3,2,0,1:T(4,128)(2,1)}), bf16[2,64,4,128]{3,2,0,1:T(4,128)(2,1)S(1)}, u32[]{:S(2)}, u32[]{:S(2)}) async-start(bf16[2,64,4,128]{3,2,0,1:T(4,128)(2,1)} %copy.75), calls=%async_computation.4 | async-start | bytes 262144 | tf_op jit(solution)/shard_map/all_to_all | solution.py:311
  94.0 8.2 %copy-start.1 = (bf16[16,1024,128]{2,1,0:T(8,128)(2,1)S(1)}, bf16[16,1024,128]{2,1,0:T(8,128)(2,1)}, u32[]{:S(2)}) copy-start(bf16[16,1024,128]{2,1,0:T(8,128)(2,1)} %get-tuple-element.42) | copy-start | bytes 12582916
  104.3 26.3 %all-to-all-start.3 = ((bf16[32,8,1024]{2,1,0:T(8,128)(2,1)}), bf16[32,8,1024]{2,1,0:T(8,128)(2,1)S(1)}, u32[]{:S(2)}, u32[]{:S(2)}) async-start(bf16[32,8,1024]{2,1,0:T(8,128)(2,1)} %fusion.2), calls=%async_computation.3 | async-start | bytes 1048576 | tf_op jit(solution)/shard_map/all_to_all | solution.py:294
Sparse Core Ops, SparseCore 0:
  27.6 40.5 all-gather.3
where the time goes:
time: 139 us; the launch traced here: 138 us
  local copies, waits for them, and re-layouts  35.6 us (26%)
  waiting for transfers between devices  31.7 us (23%)
  blocking collectives  20.5 us (15%)
  matrix products  15.7 us (11%)
  starting transfers between devices  14.9 us (11%)
  between operations  14.4 us (10%)
  other arithmetic  5.27 us (4%)
    all_gather x1, waiting for transfers between devices, exchanged(): lax.all_gather(rows.reshape(2, dp_count, tok_rows, width), ('head', 'expe...  23.2 us
    unnamed x20, local copies, waits for them, and re-layouts  17.5 us
    all_to_all x1, blocking collectives, exchanged(): rows = lax.all_to_all(rows, 'dp', split_axis=2, concat_axis=1, tiled=True)  8.64 us
    all_to_all x1, waiting for transfers between devices, exchanged(): part = lax.all_to_all(part, 'dp', split_axis=0, concat_axis=0, tiled=True)  8.55 us
    dynamic_slice x1, local copies, waits for them, and re-layouts, exchanged(): lax.dynamic_slice_in_dim(output_experts, dp_index * width, width, 1)  7.79 us
    all_gather x1, blocking collectives, exchanged(): factors = lax.all_gather(jnp.stack([value_half, outputs]), 'dp', axis=1)  6.63 us
    all_gather x1, blocking collectives, exchanged(): routes = lax.all_gather(routes, 'dp', axis=1)  5.21 us
    dot_general x2, matrix products, project(): jnp.einsum('td,pdk->tpk', source_rows, weight, preferred_element_type=jnp...  4.89 us
  transfers between devices with their start and end apart: 5, of which 2 were waited for; matrix products, arithmetic and copies ran while one was open for 25% of the time, Pallas kernels for 0%

commit v1 on v0

--- a/solution.py
+++ b/solution.py
@@ -5,6 +5,27 @@
 
 E = 4
 CAP = 3
+
+
+def ring_gather(x, axis, dim):
+    devices, position, rows = (lax.axis_size(axis), lax.axis_index(axis), x.shape[dim])
+    forward = [(i, (i + 1) % devices) for i in range(devices)]
+    behind = [(i, (i - 1) % devices) for i in range(devices)]
+    result = jnp.zeros((*x.shape[:dim], devices * rows, *x.shape[dim + 1 :]), x.dtype)
+    result = lax.dynamic_update_slice_in_dim(result, x, position * rows, axis=dim)
+    from_left = from_right = x
+    half = devices // 2
+    for lap in range(1, half + 1):
+        from_left = lax.ppermute(from_left, axis, forward)
+        result = lax.dynamic_update_slice_in_dim(
+            result, from_left, (position - lap) % devices * rows, axis=dim
+        )
+        if lap < devices - half:
+            from_right = lax.ppermute(from_right, axis, behind)
+            result = lax.dynamic_update_slice_in_dim(
+                result, from_right, (position + lap) % devices * rows, axis=dim
+            )
+    return result
 
 
 def slot_rank(routes):
@@ -221,9 +242,7 @@
     score_scale = head_dim ** (-0.5)
     rows = jnp.stack([tokens[0], cotangent[0]])
     rows = lax.all_to_all(rows, "dp", split_axis=2, concat_axis=1, tiled=True)
-    rows = lax.all_gather(
-        rows.reshape(2, dp_count, tok_rows, width), ("head", "expert"), axis=2, tiled=True
-    )
+    rows = ring_gather(rows.reshape(2, dp_count, tok_rows, width), ("head", "expert"), 2)
     token_rows = rows[0].reshape(dp_count * seq_len, width)
     cotangent_rows = rows[1].reshape(dp_count * seq_len, width)
     routes = jnp.stack([value_routes[0, :, :, 0], output_routes[0, :, :, 0]])

time: 139 us -> 133 us (0.957)
  starting transfers between devices: 14.9 us -> 33.4 us
  between operations: 14.4 us -> 0.97 us
  blocking collectives: 20.5 us -> 12.1 us
  matrix products: 15.7 us -> 13.9 us
    all_gather x1 -> x0, waiting for transfers between devices: 23.2 us -> none  [exchanged(): lax.all_gather(rows.reshape(2, dp_count, tok_rows, width), ('head', 'expe...]
    ppermute x0 -> x7, waiting for transfers between devices: none -> 17.2 us  [the longest x4 17 us: ring_gather(): from_left = lax.ppermute(from_left, axis, forward)]
    ppermute x0 -> x7, starting transfers between devices: none -> 15.3 us  [the longest x3 10.2 us: ring_gather(): from_right = lax.ppermute(from_right, axis, behind)]
    all_to_all x1 -> x0, blocking collectives: 8.64 us -> none  [exchanged(): rows = lax.all_to_all(rows, 'dp', split_axis=2, concat_axis=1, tiled=True)]
    all_to_all x0 -> x1, waiting for transfers between devices: none -> 4.66 us  [exchanged(): rows = lax.all_to_all(rows, 'dp', split_axis=2, concat_axis=1, tiled=True)]
    all_to_all x0 -> x1, starting transfers between devices: none -> 3.33 us  [exchanged(): rows = lax.all_to_all(rows, 'dp', split_axis=2, concat_axis=1, tiled=True)]
    unnamed x20 -> x14, local copies, waits for them, and re-layouts: 17.5 us -> 20.4 us
    all_to_all x1, local copies, waits for them, and re-layouts: 3.22 us -> 1.24 us  [exchanged(): rows = lax.all_to_all(rows, 'dp', split_axis=2, concat_axis=1, tiled=True)]
  transfers between devices with their start and end apart: 5 -> 12, of which waited for: 2 -> 7; matrix products, arithmetic and copies ran while one was open for 25% -> 31% of each run, Pallas kernels for 0% -> 0%
where the time goes in v1:
time: 133 us; the launch traced here: 132 us
  local copies, waits for them, and re-layouts  35.5 us (27%)
  starting transfers between devices  33.4 us (25%)
  waiting for transfers between devices  30.4 us (23%)
  matrix products  13.9 us (10%)
  blocking collectives  12.1 us (9%)
  other arithmetic  5.94 us (4%)
    unnamed x14, local copies, waits for them, and re-layouts  20.4 us
    ppermute x4, waiting for transfers between devices, ring_gather(): from_left = lax.ppermute(from_left, axis, forward)  17 us
    ppermute x3, starting transfers between devices, ring_gather(): from_right = lax.ppermute(from_right, axis, behind)  10.2 us
    all_to_all x1, waiting for transfers between devices, exchanged(): part = lax.all_to_all(part, 'dp', split_axis=0, concat_axis=0, tiled=True)  8.55 us
    dynamic_slice x1, local copies, waits for them, and re-layouts, exchanged(): lax.dynamic_slice_in_dim(output_experts, dp_index * width, width, 1)  7.77 us
    all_gather x1, blocking collectives, exchanged(): factors = lax.all_gather(jnp.stack([value_half, outputs]), 'dp', axis=1)  6.63 us
    all_gather x1, blocking collectives, exchanged(): routes = lax.all_gather(routes, 'dp', axis=1)  5.48 us
    ppermute x4, starting transfers between devices, ring_gather(): from_left = lax.ppermute(from_left, axis, forward)  5.05 us
  transfers between devices with their start and end apart: 12, of which 7 were waited for; matrix products, arithmetic and copies ran while one was open for 31% of the time, Pallas kernels for 0%

profile of v1, /device:TPU:0, one launch (start us, length us, event | category | flops | bytes accessed | tf_op | source)
XLA Modules:
  0.0 132.2 jit_solution(13692916528958874912)
XLA Ops:
  3.0 4.3 %all-to-all-start.2 = ((bf16[2,32,8,128]{3,1,0,2:T(8,128)(2,1)}), bf16[2,32,8,128]{3,1,0,2:T(8,128)(2,1)S(1)}, u32[]{:S(2)}, u32[]{:S(2)}) async-start(bf16[2,32,8,128]{3,1,0,2:T(8,128)(2,1)} %pad_maximum_fusion.1), calls=%async_computation.2 | async-start | bytes 262144 | tf_op jit(solution)/shard_map/all_to_all | solution.py:254
  8.0 5.5 %all-gather = s32[2,16,64]{2,0,1:T(2,128)S(1)} all-gather(s32[2,4,64]{2,0,1:T(2,128)S(1)} %fusion.17), channel_id=2, replica_groups=mesh['dp'=4,'head'=4,'expert'=2] {'dp'}, dimensions={1}, use_global_device_ids=true | all-gather | bytes 10240 | tf_op jit(solution)/shard_map/all_gather | solution.py:250
  14.7 2.8 %copy.61 = bf16[2,8,4096]{1,0,2:T(2,128)(2,1)S(1)} copy(bf16[2,8,4096]{2,1,0:T(8,128)(2,1)S(1)} %pad_maximum_fusion.2) | data formatting | bytes 262144 | tf_op jit(solution)/shard_map/stack | solution.py:243
  17.5 2.8 %reshape.83 = bf16[4,2,8192]{2,1,0:T(2,128)(2,1)} reshape(bf16[4096,2,8]{2,1,0:T(2,128)(2,1)S(1)} %bitcast.117) | data formatting | bytes 262144
  20.3 7.8 %constant_dynamic-slice_fusion = (bf16[16,1024,128]{2,1,0:T(8,128)(2,1)}, bf16[16,1024,128]{2,1,0:T(8,128)(2,1)}) fusion(bf16[16,4096,128]{2,1,0:T(8,128)(2,1)} %param.15, s32[]{:T(128)S(6)} %select_n.96, bf16[16,4096,128]{2,1,0:T(8,128)(2,1)} %param.14), kind=kLoop, calls=%fused_computation.48 | loop fusion | bytes 16777220 | tf_op jit(solution)/shard_map/dynamic_slice | solution.py:257
  28.1 3.3 %all-to-all-start = ((bf16[4,2,8192]{2,1,0:T(2,128)(2,1)}), bf16[4,2,8192]{2,1,0:T(2,128)(2,1)S(1)}, u32[]{:S(2)}, u32[]{:S(2)}) async-start(bf16[4,2,8192]{2,1,0:T(2,128)(2,1)} %reshape.83), calls=%async_computation | async-start | bytes 262144 | tf_op jit(solution)/shard_map/all_to_all | solution.py:244
  31.5 4.7 %all-to-all-done = bf16[4,2,8192]{2,1,0:T(2,128)(2,1)S(1)} async-done(((bf16[4,2,8192]{2,1,0:T(2,128)(2,1)}), bf16[4,2,8192]{2,1,0:T(2,128)(2,1)S(1)}, u32[]{:S(2)}, u32[]{:S(2)}) %all-to-all-start) | async-done | bytes 131104 | tf_op jit(solution)/shard_map/all_to_all | solution.py:244
  36.1 2.4 %reshape.84 = bf16[4096,2,8]{2,1,0:T(2,128)(2,1)S(1)} reshape(bf16[4,2,8192]{2,1,0:T(2,128)(2,1)S(1)} %all-to-all-done) | data formatting | bytes 262144
  41.8 3.4 %collective-permute-start.1 = (bf16[2,4,8,1024]{3,2,1,0:T(8,128)(2,1)S(1)}, bf16[2,4,8,1024]{3,2,1,0:T(8,128)(2,1)S(1)}, u32[]{:S(2)}, u32[]{:S(2)}) collective-permute-start(bf16[2,4,8,1024]{3,2,1,0:T(8,128)(2,1)S(1)} %bitcast.133), channel_id=1, source_target_pairs={{0,7},{1,0},{2,1},{3,2},{4,3},{5,4},{6,5},{7,6},{8,15},{9,8},{10,9... | collective-permute-start | bytes 393224 | tf_op jit(solution)/shard_map/ppermute | solution.py:24
  45.3 3.0 %collective-permute-done = bf16[2,4,8,1024]{3,2,1,0:T(8,128)(2,1)S(1)} collective-permute-done((bf16[2,4,8,1024]{3,2,1,0:T(8,128)(2,1)S(1)}, bf16[2,4,8,1024]{3,2,1,0:T(8,128)(2,1)S(1)}, u32[]{:S(2)}, u32[]{:S(2)}) %collective-permute-start) | collective-permute-done | bytes 131104 | tf_op jit(solution)/shard_map/ppermute | solution.py:19
  49.5 3.5 %collective-permute-start.3 = (bf16[2,4,8,1024]{3,2,1,0:T(8,128)(2,1)S(1)}, bf16[2,4,8,1024]{3,2,1,0:T(8,128)(2,1)S(1)}, u32[]{:S(2)}, u32[]{:S(2)}) collective-permute-start(bf16[2,4,8,1024]{3,2,1,0:T(8,128)(2,1)S(1)} %collective-permute-done.1), channel_id=1, source_target_pairs={{0,7},{1,0},{2,1},{3,2},{4,3},{5,4},{6,5},{7,6},{8,15},{9,8},{10,9... | collective-permute-start | bytes 393224 | tf_op jit(solution)/shard_map/ppermute | solution.py:24
  53.1 3.0 %collective-permute-done.2 = bf16[2,4,8,1024]{3,2,1,0:T(8,128)(2,1)S(1)} collective-permute-done((bf16[2,4,8,1024]{3,2,1,0:T(8,128)(2,1)S(1)}, bf16[2,4,8,1024]{3,2,1,0:T(8,128)(2,1)S(1)}, u32[]{:S(2)}, u32[]{:S(2)}) %collective-permute-start.2) | collective-permute-done | bytes 131104 | tf_op jit(solution)/shard_map/ppermute | solution.py:19
  57.6 3.3 %collective-permute-start.5 = (bf16[2,4,8,1024]{3,2,1,0:T(8,128)(2,1)S(1)}, bf16[2,4,8,1024]{3,2,1,0:T(8,128)(2,1)S(1)}, u32[]{:S(2)}, u32[]{:S(2)}) collective-permute-start(bf16[2,4,8,1024]{3,2,1,0:T(8,128)(2,1)S(1)} %collective-permute-done.3), channel_id=1, source_target_pairs={{0,7},{1,0},{2,1},{3,2},{4,3},{5,4},{6,5},{7,6},{8,15},{9,8},{10,9... | collective-permute-start | bytes 393224 | tf_op jit(solution)/shard_map/ppermute | solution.py:24
  61.0 3.0 %collective-permute-done.4 = bf16[2,4,8,1024]{3,2,1,0:T(8,128)(2,1)S(1)} collective-permute-done((bf16[2,4,8,1024]{3,2,1,0:T(8,128)(2,1)S(1)}, bf16[2,4,8,1024]{3,2,1,0:T(8,128)(2,1)S(1)}, u32[]{:S(2)}, u32[]{:S(2)}) %collective-permute-start.4) | collective-permute-done | bytes 131104 | tf_op jit(solution)/shard_map/ppermute | solution.py:19
  64.6 8.0 %collective-permute-done.6 = bf16[2,4,8,1024]{3,2,1,0:T(8,128)(2,1)S(1)} collective-permute-done((bf16[2,4,8,1024]{3,2,1,0:T(8,128)(2,1)S(1)}, bf16[2,4,8,1024]{3,2,1,0:T(8,128)(2,1)S(1)}, u32[]{:S(2)}, u32[]{:S(2)}) %collective-permute-start.6) | collective-permute-done | bytes 131104 | tf_op jit(solution)/shard_map/ppermute | solution.py:19
  78.0 3.5 %all-to-all-start.1 = ((bf16[4,2,64,4,128]{4,3,2,1,0:T(4,128)(2,1)}), bf16[4,2,64,4,128]{4,3,2,1,0:T(4,128)(2,1)S(1)}, u32[]{:S(2)}, u32[]{:S(2)}) async-start(bf16[4,2,64,4,128]{4,3,2,1,0:T(4,128)(2,1)} %pad_maximum_fusion), calls=%async_computation.1 | async-start | bytes 1048576 | tf_op jit(solution)/shard_map/all_to_all | solution.py:275
  81.7 8.6 %all-to-all-done.1 = bf16[4,2,64,4,128]{4,3,2,1,0:T(4,128)(2,1)S(1)} async-done(((bf16[4,2,64,4,128]{4,3,2,1,0:T(4,128)(2,1)}), bf16[4,2,64,4,128]{4,3,2,1,0:T(4,128)(2,1)S(1)}, u32[]{:S(2)}, u32[]{:S(2)}) %all-to-all-start.1) | async-done | bytes 524320 | tf_op jit(solution)/shard_map/all_to_all | solution.py:275
  92.5 3.4 %all-to-all-start.4 = ((bf16[2,64,4,128]{3,2,0,1:T(4,128)(2,1)}), bf16[2,64,4,128]{3,2,0,1:T(4,128)(2,1)S(1)}, u32[]{:S(2)}, u32[]{:S(2)}) async-start(bf16[2,64,4,128]{3,2,0,1:T(4,128)(2,1)} %copy.75), calls=%async_computation.4 | async-start | bytes 262144 | tf_op jit(solution)/shard_map/all_to_all | solution.py:330
  95.9 6.6 %all-gather.1 = bf16[2,256,4,128]{3,1,2,0:T(8,128)(2,1)S(1)} all-gather(bf16[2,64,4,128]{3,1,2,0:T(8,128)(2,1)S(1)} %pad_maximum_fusion.3), channel_id=3, replica_groups=mesh['dp'=4,'head'=4,'expert'=2] {'dp'}, dimensions={1}, use_global_device_ids=true | all-gather | bytes 655360 | tf_op jit(solution)/shard_map/all_gather | solution.py:305
  106.2 3.6 %all-to-all-start.3 = ((bf16[32,8,1024]{2,1,0:T(8,128)(2,1)}), bf16[32,8,1024]{2,1,0:T(8,128)(2,1)S(1)}, u32[]{:S(2)}, u32[]{:S(2)}) async-start(bf16[32,8,1024]{2,1,0:T(8,128)(2,1)} %fusion.2), calls=%async_computation.3 | async-start | bytes 1048576 | tf_op jit(solution)/shard_map/all_to_all | solution.py:313
  109.8 4.3 %convert_bitcast_fusion = bf16[16,1024,128]{1,2,0:T(8,128)(2,1)} fusion(bf16[256,16,128]{2,0,1:T(8,128)(2,1)S(1)} %bitcast.123, bf16[256,1024,1]{1,0,2:T(8,128)(2,1)} %bitcast.127), kind=kOutput, calls=%fused_computation.1 | convolution fusion | flops 1075838976 | bytes 5767168 | tf_op jit(solution)/shard_map/td,tpk->pdk/dot_general | solution.py:327
  114.2 6.4 %copy.81 = bf16[16,1024,128]{2,1,0:T(8,128)(2,1)} copy(bf16[16,1024,128]{1,2,0:T(8,128)(2,1)} %convert_bitcast_fusion) | data formatting | bytes 8388608
  120.6 3.2 %convert_bitcast_fusion.1 = bf16[16,1024,128]{1,2,0:T(8,128)(2,1)} fusion(bf16[256,16,128]{2,0,1:T(8,128)(2,1)S(1)} %bitcast.122, bf16[256,1024,1]{1,0,2:T(8,128)(2,1)S(1)} %bitcast.125), kind=kOutput, calls=%fused_computation.2 | convolution fusion | flops 1075838976 | bytes 5767168 | tf_op jit(solution)/shard_map/td,tpk->pdk/dot_general | solution.py:324
  123.8 6.4 %copy.80 = bf16[16,1024,128]{2,1,0:T(8,128)(2,1)} copy(bf16[16,1024,128]{1,2,0:T(8,128)(2,1)} %convert_bitcast_fusion.1) | data formatting | bytes 8388608
  (68 shorter events, 24.4 us)
Async XLA Ops:
  3.0 25.1 %all-to-all-start.2 = ((bf16[2,32,8,128]{3,1,0,2:T(8,128)(2,1)}), bf16[2,32,8,128]{3,1,0,2:T(8,128)(2,1)S(1)}, u32[]{:S(2)}, u32[]{:S(2)}) async-start(bf16[2,32,8,128]{3,1,0,2:T(8,128)(2,1)} %pad_maximum_fusion.1), calls=%async_computation.2 | async-start | bytes 262144 | tf_op jit(solution)/shard_map/all_to_all | solution.py:254
  28.1 8.0 %all-to-all-start = ((bf16[4,2,8192]{2,1,0:T(2,128)(2,1)}), bf16[4,2,8192]{2,1,0:T(2,128)(2,1)S(1)}, u32[]{:S(2)}, u32[]{:S(2)}) async-start(bf16[4,2,8192]{2,1,0:T(2,128)(2,1)} %reshape.83), calls=%async_computation | async-start | bytes 262144 | tf_op jit(solution)/shard_map/all_to_all | solution.py:244
  39.8 32.9 %copy-start.2 = (bf16[16,1024,128]{2,1,0:T(8,128)(2,1)S(1)}, bf16[16,1024,128]{2,1,0:T(8,128)(2,1)}, u32[]{:S(2)}) copy-start(bf16[16,1024,128]{2,1,0:T(8,128)(2,1)} %get-tuple-element.41) | copy-start | bytes 12582916
  39.8 8.5 %collective-permute-start = (bf16[2,4,8,1024]{3,2,1,0:T(8,128)(2,1)S(1)}, bf16[2,4,8,1024]{3,2,1,0:T(8,128)(2,1)S(1)}, u32[]{:S(2)}, u32[]{:S(2)}) collective-permute-start(bf16[2,4,8,1024]{3,2,1,0:T(8,128)(2,1)S(1)} %bitcast.132), channel_id=1, source_target_pairs={{0,1},{1,2},{2,3},{3,4},{4,5},{5,6},{6,7},{7,0},{8,9},{9,10},{10,1... | collective-permute-start | bytes 393224 | tf_op jit(solution)/shard_map/ppermute | solution.py:19
  41.8 7.8 %collective-permute-start.1 = (bf16[2,4,8,1024]{3,2,1,0:T(8,128)(2,1)S(1)}, bf16[2,4,8,1024]{3,2,1,0:T(8,128)(2,1)S(1)}, u32[]{:S(2)}, u32[]{:S(2)}) collective-permute-start(bf16[2,4,8,1024]{3,2,1,0:T(8,128)(2,1)S(1)} %bitcast.133), channel_id=1, source_target_pairs={{0,7},{1,0},{2,1},{3,2},{4,3},{5,4},{6,5},{7,6},{8,15},{9,8},{10,9... | collective-permute-start | bytes 393224 | tf_op jit(solution)/shard_map/ppermute | solution.py:24
  48.3 7.8 %collective-permute-start.2 = (bf16[2,4,8,1024]{3,2,1,0:T(8,128)(2,1)S(1)}, bf16[2,4,8,1024]{3,2,1,0:T(8,128)(2,1)S(1)}, u32[]{:S(2)}, u32[]{:S(2)}) collective-permute-start(bf16[2,4,8,1024]{3,2,1,0:T(8,128)(2,1)S(1)} %collective-permute-done), channel_id=1, source_target_pairs={{0,1},{1,2},{2,3},{3,4},{4,5},{5,6},{6,7},{7,0},{8,9},{9,10},{10,1... | collective-permute-start | bytes 393224 | tf_op jit(solution)/shard_map/ppermute | solution.py:19
  49.5 8.1 %collective-permute-start.3 = (bf16[2,4,8,1024]{3,2,1,0:T(8,128)(2,1)S(1)}, bf16[2,4,8,1024]{3,2,1,0:T(8,128)(2,1)S(1)}, u32[]{:S(2)}, u32[]{:S(2)}) collective-permute-start(bf16[2,4,8,1024]{3,2,1,0:T(8,128)(2,1)S(1)} %collective-permute-done.1), channel_id=1, source_target_pairs={{0,7},{1,0},{2,1},{3,2},{4,3},{5,4},{6,5},{7,6},{8,15},{9,8},{10,9... | collective-permute-start | bytes 393224 | tf_op jit(solution)/shard_map/ppermute | solution.py:24
  56.1 7.9 %collective-permute-start.4 = (bf16[2,4,8,1024]{3,2,1,0:T(8,128)(2,1)S(1)}, bf16[2,4,8,1024]{3,2,1,0:T(8,128)(2,1)S(1)}, u32[]{:S(2)}, u32[]{:S(2)}) collective-permute-start(bf16[2,4,8,1024]{3,2,1,0:T(8,128)(2,1)S(1)} %collective-permute-done.2), channel_id=1, source_target_pairs={{0,1},{1,2},{2,3},{3,4},{4,5},{5,6},{6,7},{7,0},{8,9},{9,10},{10,1... | collective-permute-start | bytes 393224 | tf_op jit(solution)/shard_map/ppermute | solution.py:19
  57.6 6.9 %collective-permute-start.5 = (bf16[2,4,8,1024]{3,2,1,0:T(8,128)(2,1)S(1)}, bf16[2,4,8,1024]{3,2,1,0:T(8,128)(2,1)S(1)}, u32[]{:S(2)}, u32[]{:S(2)}) collective-permute-start(bf16[2,4,8,1024]{3,2,1,0:T(8,128)(2,1)S(1)} %collective-permute-done.3), channel_id=1, source_target_pairs={{0,7},{1,0},{2,1},{3,2},{4,3},{5,4},{6,5},{7,6},{8,15},{9,8},{10,9... | collective-permute-start | bytes 393224 | tf_op jit(solution)/shard_map/ppermute | solution.py:24
  64.0 8.6 %collective-permute-start.6 = (bf16[2,4,8,1024]{3,2,1,0:T(8,128)(2,1)S(1)}, bf16[2,4,8,1024]{3,2,1,0:T(8,128)(2,1)S(1)}, u32[]{:S(2)}, u32[]{:S(2)}) collective-permute-start(bf16[2,4,8,1024]{3,2,1,0:T(8,128)(2,1)S(1)} %collective-permute-done.4), channel_id=1, source_target_pairs={{0,1},{1,2},{2,3},{3,4},{4,5},{5,6},{6,7},{7,0},{8,9},{9,10},{10,1... | collective-permute-start | bytes 393224 | tf_op jit(solution)/shard_map/ppermute | solution.py:19
  72.7 3.9 %copy-start.3 = (bf16[1,4,64,1024]{3,2,1,0:T(8,128)(2,1)}, bf16[1,4,64,1024]{3,2,1,0:T(8,128)(2,1)S(1)}, u32[]{:S(2)}) copy-start(bf16[1,4,64,1024]{3,2,1,0:T(8,128)(2,1)S(1)} %get-tuple-element.28) | copy-start | bytes 1572868
  72.7 2.4 %copy-start = (bf16[16,1024,128]{2,1,0:T(8,128)(2,1)S(1)}, bf16[16,1024,128]{2,1,0:T(8,128)(2,1)}, u32[]{:S(2)}) copy-start(bf16[16,1024,128]{2,1,0:T(8,128)(2,1)} %get-tuple-element.42) | copy-start | bytes 12582916
  78.0 12.3 %all-to-all-start.1 = ((bf16[4,2,64,4,128]{4,3,2,1,0:T(4,128)(2,1)}), bf16[4,2,64,4,128]{4,3,2,1,0:T(4,128)(2,1)S(1)}, u32[]{:S(2)}, u32[]{:S(2)}) async-start(bf16[4,2,64,4,128]{4,3,2,1,0:T(4,128)(2,1)} %pad_maximum_fusion), calls=%async_computation.1 | async-start | bytes 1048576 | tf_op jit(solution)/shard_map/all_to_all | solution.py:275
  92.5 13.7 %all-to-all-start.4 = ((bf16[2,64,4,128]{3,2,0,1:T(4,128)(2,1)}), bf16[2,64,4,128]{3,2,0,1:T(4,128)(2,1)S(1)}, u32[]{:S(2)}, u32[]{:S(2)}) async-start(bf16[2,64,4,128]{3,2,0,1:T(4,128)(2,1)} %copy.75), calls=%async_computation.4 | async-start | bytes 262144 | tf_op jit(solution)/shard_map/all_to_all | solution.py:330
  95.9 8.2 %copy-start.1 = (bf16[16,1024,128]{2,1,0:T(8,128)(2,1)S(1)}, bf16[16,1024,128]{2,1,0:T(8,128)(2,1)}, u32[]{:S(2)}) copy-start(bf16[16,1024,128]{2,1,0:T(8,128)(2,1)} %get-tuple-element.42) | copy-start | bytes 12582916
  106.2 25.3 %all-to-all-start.3 = ((bf16[32,8,1024]{2,1,0:T(8,128)(2,1)}), bf16[32,8,1024]{2,1,0:T(8,128)(2,1)S(1)}, u32[]{:S(2)}, u32[]{:S(2)}) async-start(bf16[32,8,1024]{2,1,0:T(8,128)(2,1)} %fusion.2), calls=%async_computation.3 | async-start | bytes 1048576 | tf_op jit(solution)/shard_map/all_to_all | solution.py:313
